TPU v7x, 32 devices: a whole 2x2x4 slice. The times are simulated.
32 devices in a mesh: ew: 8 (over z, x), ns: 4 (over y, core).
Axes of the slice: x: 2, y: 2, z: 4, core: 2. Of those that a mesh axis runs over, the one named last changes fastest.
Arguments:
- grid: bfloat16 [8, 2, 1280, 5136], P(None, None, 'ns', 'ew'), may hold values from -6 to 6
- band_rows: int32 [1280], replicated, may hold values from 0 to 1279, each once
- wave_pairs: int32 [4], replicated, may hold values from 0 to 323, as said below
- packer_order: int32 [8], replicated, may hold values from 0 to 7, each once
- field_bits: int32 [4], replicated, may hold values from 10 to 14
- field_power: float32 [4], replicated, may hold values from -0.6 to 0.6
- legendre: float32 [4, 1280, 649], P('ns'), may hold values from -0.15625 to 0.15625
Outputs:
- packed: float32 [8, 4, 2, 649], P('ew', 'ns')
Inputs may be any that keep to these rules, and one draw needn't show every extreme that they name: `wave_pairs`: distinct values.
All inputs are finite; a program needn't handle non-finite values.
Results may differ from a plain program's by a relative error of at most 0.0003.
Values sent between devices are 32-bit elements; how exact they have to be, the bound alone decides.
No kernel may reach another device: no remote copies, remote signals or barrier semaphores. Data moves between devices by JAX's collectives and lax.ppermute only.
A program may use at most 128 MiB of HBM per device.

v0:
```python
import jax
import jax.numpy as jnp
from jax import lax
from jax.sharding import PartitionSpec as P


def cycle_table(lat_ids, first_point, point_count, wave_list, truncation):
    lengths = 20 + 4 * lat_ids
    points = first_point + jnp.arange(point_count, dtype=jnp.int32)
    numbers = jnp.stack([wave_list, truncation - wave_list], 1).reshape(-1)
    product = numbers[None, None, :] * points[None, :, None] % lengths[:, None, None]
    length_f = lengths.astype(jnp.float32)[:, None, None]
    angles = product.astype(jnp.float32) * (6.283185307179586 / length_f)
    inside = points[None, :, None] < lengths[:, None, None]
    factor = jnp.where(inside, 1.0 / length_f, jnp.float32(0.0))
    trig_values = jnp.stack([jnp.cos(angles) * factor, -jnp.sin(angles) * factor], -1)
    return trig_values.reshape(lat_ids.shape[0], point_count, -1)


def coefficients(ordered, legendre, wave_list, truncation, powers):
    symmetric = ordered[:, 0] + ordered[:, 1]
    antisym = ordered[:, 0] - ordered[:, 1]
    slots, nlat, width = symmetric.shape
    pcount = width // 4
    stacked = jnp.concatenate(
        [symmetric.reshape(slots, nlat, pcount, 4), antisym.reshape(slots, nlat, pcount, 4)], -1
    )
    result = jnp.einsum("prc,frpq->fpqc", legendre, stacked, precision=lax.Precision.HIGHEST)
    columns = jnp.arange(legendre.shape[2], dtype=jnp.int32)[None, :]
    wavenum = wave_list[:, None]
    first_part = columns <= truncation - wavenum
    shifted = columns - (truncation - wavenum + 1)
    even_parity = jnp.where(first_part, columns % 2 == 0, shifted % 2 == 0)
    halves = []
    for e in (0, 1):
        chosen = jnp.where(
            first_part,
            jnp.where(even_parity, result[:, :, e], result[:, :, 4 + e]),
            jnp.where(even_parity, result[:, :, 2 + e], result[:, :, 6 + e]),
        )
        halves.append(chosen)
    coefficient = jnp.stack(halves, 2)
    degree = jnp.where(first_part, wavenum + columns, columns - 1).astype(jnp.float32)
    logs = jnp.log(degree * (degree + 1.0) + 2.0)
    weight = jnp.exp(powers[:, None, None] * logs[None, :, :])
    return coefficient * weight[:, :, None, :]


def slot_settings(slot_fields, field_bits, field_power, levels):
    field_type = slot_fields // levels
    onehot = field_type[:, None] == jnp.arange(field_bits.shape[0], dtype=jnp.int32)[None, :]
    powers = jnp.sum(jnp.where(onehot, field_power[None, :], jnp.float32(0.0)), -1)
    bit_count = jnp.sum(jnp.where(onehot, field_bits[None, :], 0), -1).astype(jnp.float32)
    return (powers, (jnp.exp2(bit_count) - 1.0) / 4096.0)


def pack_values(scaled, lowest, highest, spread):
    span = highest - lowest + 1e-06
    return (
        (scaled - lowest[:, None, None, None])
        / span[:, None, None, None]
        * spread[:, None, None, None]
    )


def segment_terms_of(picked_rows, trig_values):
    return jnp.einsum(
        "fhrk,rkc->fhrc",
        picked_rows.astype(jnp.float32),
        trig_values,
        precision=lax.Precision.HIGHEST,
    )


def shards(grid, band_rows, wave_pairs, packer_order, field_bits, field_power, legendre):
    band_size = grid.shape[2]
    segment = grid.shape[3]
    total_slots = grid.shape[0]
    fl_dev = total_slots // lax.axis_size("ew")
    pair_dev = legendre.shape[0]
    truncation = legendre.shape[2] - 2
    levels = total_slots // field_bits.shape[0]
    ns_index = lax.axis_index("ns")
    ew_index = lax.axis_index("ew")
    lat_ids = lax.dynamic_slice_in_dim(band_rows, ns_index * band_size, band_size)
    trig_values = cycle_table(lat_ids, ew_index * segment, segment, wave_pairs, truncation)
    summed = lax.psum_scatter(
        segment_terms_of(jnp.take(grid, packer_order, axis=0), trig_values),
        "ew",
        scatter_dimension=0,
        tiled=True,
    )
    ordered = lax.all_to_all(summed, "ns", split_axis=3, concat_axis=2, tiled=True)
    local_waves = lax.dynamic_slice_in_dim(wave_pairs, ns_index * pair_dev, pair_dev)
    local_fields = lax.dynamic_slice_in_dim(packer_order, ew_index * fl_dev, fl_dev)
    powers, spread = slot_settings(local_fields, field_bits, field_power, levels)
    scaled = coefficients(ordered, legendre, local_waves, truncation, powers)
    local_high = jnp.max(scaled, axis=(1, 2, 3))
    local_low = jnp.min(scaled, axis=(1, 2, 3))
    highest = lax.pmax(local_high, "ns")
    lowest = lax.pmin(local_low, "ns")
    return pack_values(scaled, lowest, highest, spread)


def solution(mesh):
    return jax.shard_map(
        shards,
        mesh=mesh,
        in_specs=(P(None, None, "ns", "ew"), P(), P(), P(), P(), P(), P("ns", None, None)),
        out_specs=P("ew", "ns", None, None),
        check_vma=False,
    )
```

profile of v0, /device:TPU:0, one launch (start us, length us, event | category | flops | bytes accessed | tf_op | source)
XLA Modules:
  0.0 291.0 jit_solution(4864058309195393743)
XLA Ops:
  6.5 0.0 reduce-scatter.2.cloned.1.call-start
  6.5 0.8 broadcast_compare_fusion
  7.3 0.7 compare_select_fusion.5
  8.0 0.7 compare_and_fusion
  8.7 0.7 subtract_bitcast_fusion.1
  9.3 0.7 pad_add_fusion
  10.0 0.1 copy.24
  10.1 0.1 mul.142
  10.2 0.2 compare_select_fusion
  10.3 0.1 broadcast_multiply_fusion
  10.4 107.2 %fusion.6 = (f32[320,642,8,1]{1,2,3,0:T(8,128)}, f32[320,642,8,1]{1,2,3,0:T(8,128)}) fusion(f32[320,642]{1,0:T(8,128)S(1)} %compare_select_fusion, f32[320]{0:T(512)S(1)} %get-tuple-element.16, s32[320]{0:T(512)S(1)} %compare_select_fusion.4, s32[642,8]{0,1:T(8,128)S(1)} %broadcast_multiply_fusion, pred[320]{0:T(512)(128)(4,1)S(1)} %get-tuple-element.8), kind=kLoop, calls=%fused_computation.12 | loop fusion | flops 19722240 | bytes 13993344 | tf_op jit(solution)/shard_map/mul | solution.py:16
  117.6 12.5 %pad_maximum_fusion = f32[320,642,8,2]{1,2,3,0:T(8,128)} fusion(f32[320,642,8,1]{1,2,3,0:T(8,128)} %get-tuple-element.11, f32[320,642,8,1]{1,2,3,0:T(8,128)} %get-tuple-element.10), kind=kLoop, calls=%fused_computation.5 | loop fusion | flops 3287040 | bytes 26296320 | tf_op jit(solution)/shard_map/stack | solution.py:16
  130.1 20.1 %copy.25 = f32[320,642,8,2]{1,0,3,2:T(8,128)} copy(f32[320,642,8,2]{1,2,3,0:T(8,128)} %pad_maximum_fusion) | data formatting | bytes 26296320 | tf_op jit(solution)/shard_map/stack | solution.py:16
  150.1 7.7 %gather_fusion = bf16[8,2,320,642]{3,2,1,0:T(8,128)(2,1)} fusion(bf16[8,2,320,642]{3,2,1,0:T(8,128)(2,1)} %param.7, s32[1024]{0:T(1024)S(1)} %pad_clamp_fusion), kind=kCustom, calls=%fused_computation | custom fusion | bytes 13148192 | tf_op jit(solution)/shard_map/jit(_take)/gather | solution.py:88
  157.9 4.1 %broadcast_select_fusion = bf16[8,2,320,642]{3,2,1,0:T(8,128)(2,1)S(1)} fusion(bf16[8,2,320,642]{3,2,1,0:T(8,128)(2,1)} %gather_fusion, pred[8]{0:T(512)(128)(4,1)S(1)} %compare_and_fusion), kind=kLoop, calls=%fused_computation.16 | loop fusion | flops 3287040 | bytes 13148168 | tf_op jit(solution)/shard_map/jit(_take)/select_n | solution.py:88
  161.9 0.0 copy-start.1
  161.9 0.0 copy-start
  162.0 0.0 copy-start.2
  162.0 0.0 copy-start.3
  162.0 23.8 %fusion.15 = f32[8,2,320,16]{3,0,1,2:T(8,128)} fusion(bf16[8,2,320,642]{3,2,1,0:T(8,128)(2,1)S(1)} %broadcast_select_fusion, f32[320,642,16,1]{1,0,2,3:T(8,128)} %bitcast.35), kind=kOutput, calls=%fused_computation.22 | convolution fusion | flops 631111680 | bytes 20049920 | tf_op jit(solution)/shard_map/fhrk,rkc->fhrc/dot_general | solution.py:67
  185.8 3.6 %copy.28 = f32[8,2,320,16]{2,3,1,0:T(8,128)} copy(f32[8,2,320,16]{3,0,1,2:T(8,128)} %fusion.15) | data formatting | bytes 655360 | tf_op jit(solution)/shard_map/fhrk,rkc->fhrc/transpose | solution.py:67
  189.4 0.0 reduce-scatter.2.cloned.1.call-update
  189.4 0.0 copy-done.1
  189.4 0.6 dynamic_slice.11
  192.6 0.0 copy-done
  192.6 0.6 dynamic_slice.9
  193.9 0.0 copy-done.2
  193.9 0.7 fusion.32
  194.5 0.0 copy-done.3
  194.5 0.7 fusion.33
  195.3 59.2 %reduce-scatter.2.cloned.1.call-done = f32[1,2,320,16]{2,3,1,0:T(8,128)} async-done(((f32[8,2,320,16]{2,3,1,0:T(8,128)}), f32[1,2,320,16]{2,3,1,0:T(8,128)}) %reduce-scatter.2.cloned.1.call-update) | async-done | bytes 40976 | tf_op jit(solution)/shard_map/reduce_scatter | solution.py:87
  254.4 1.4 copy.29
  255.9 3.3 %all-to-all-start = ((f32[1,2,320,16]{2,1,0,3:T(2,128)}), f32[1,2,320,16]{2,1,0,3:T(2,128)S(1)}, u32[]{:S(2)}, u32[]{:S(2)}) async-start(f32[1,2,320,16]{2,1,0,3:T(2,128)} %copy.29), calls=%async_computation.1 | async-start | bytes 98304 | tf_op jit(solution)/shard_map/all_to_all | solution.py:93
  259.1 1.3 fusion.28
  261.9 1.3 all-to-all-done
  263.1 0.1 all_to_all.16
  263.3 4.8 %fusion.20 = f32[1,1,8,649]{3,2,1,0:T(8,128)S(1)} fusion(f32[1,1280,649]{1,0,2:T(1,128)} %param.13, f32[1,1280,1,4]{1,3,2,0:T(4,128)S(1)} %get-tuple-element.13, f32[1,1280,1,4]{1,3,2,0:T(4,128)S(1)} %get-tuple-element.12), kind=kOutput, calls=%fused_computation.23 | convolution fusion | flops 79759360 | bytes 3384608 | tf_op jit(solution)/shard_map/prc,frpq->fpqc/dot_general | solution.py:28
  268.0 0.1 fusion.31
  268.1 0.6 fusion.35
  268.7 6.8 %pmax.7 = f32[1]{0:T(128)} all-reduce(f32[1]{0:T(128)} %bitcast.17), channel_id=1, replica_groups=mesh['ew'=8,'ns'=4] {'ns'}, use_global_device_ids=true, to_apply=%region_5.6 | all-reduce | flops 1 | bytes 8 | tf_op jit(solution)/shard_map/pmax | solution.py:100
  275.5 6.3 %pmin.7 = f32[1]{0:T(128)} all-reduce(f32[1]{0:T(128)} %bitcast.15), channel_id=1, replica_groups=mesh['ew'=8,'ns'=4] {'ns'}, use_global_device_ids=true, to_apply=%region_3.4 | all-reduce | flops 1 | bytes 8 | tf_op jit(solution)/shard_map/pmin | solution.py:101
  283.0 1.2 divide_multiply_fusion
  (6 shorter events, 0.0 us)
Async XLA Ops:
  6.5 247.9 %reduce-scatter.2.cloned.1.call-start = ((), (), s32[]{:S(2)}) async-start(), calls=%async_computation.2 | async-start | bytes 442368 | tf_op jit(solution)/shard_map/reduce_scatter | solution.py:87
  161.9 27.5 %copy-start.1 = (s32[8]{0:T(128)S(1)}, s32[8]{0:T(128)}, u32[]{:S(2)}) copy-start(s32[8]{0:T(128)} %param.10) | copy-start | bytes 100
  161.9 30.7 %copy-start = (s32[4]{0:T(128)S(1)}, s32[4]{0:T(128)}, u32[]{:S(2)}) copy-start(s32[4]{0:T(128)} %param.9) | copy-start | bytes 52
  162.0 31.9 %copy-start.2 = (f32[4]{0:T(128)S(1)}, f32[4]{0:T(128)}, u32[]{:S(2)}) copy-start(f32[4]{0:T(128)} %param.12) | copy-start | bytes 52
  162.0 32.6 %copy-start.3 = (s32[4]{0:T(128)S(1)}, s32[4]{0:T(128)}, u32[]{:S(2)}) copy-start(s32[4]{0:T(128)} %param.11) | copy-start | bytes 52
  255.9 7.3 %all-to-all-start = ((f32[1,2,320,16]{2,1,0,3:T(2,128)}), f32[1,2,320,16]{2,1,0,3:T(2,128)S(1)}, u32[]{:S(2)}, u32[]{:S(2)}) async-start(f32[1,2,320,16]{2,1,0,3:T(2,128)} %copy.29), calls=%async_computation.1 | async-start | bytes 98304 | tf_op jit(solution)/shard_map/all_to_all | solution.py:93
Sparse Core Ops, SparseCore 0:
  189.5 64.8 reduce-scatter.1
where the time goes:
time: 292 us; the launch traced here: 291 us
  other arithmetic  132 us (45%)
  waiting for transfers between devices  60.4 us (21%)
  local copies, waits for them, and re-layouts  34.3 us (12%)
  matrix products  28.6 us (10%)
  between operations  19.4 us (7%)
  blocking collectives  13 us (4%)
  starting transfers between devices  3.27 us (1%)
    mul x1, other arithmetic, cycle_table(): jnp.cos(angles) * factor  107 us
    reduce_scatter x1, waiting for transfers between devices, shards(): lax.psum_scatter(segment_terms_of(jnp.take(grid, packer_order, axis=0), t...  59.2 us
    dot_general x1, matrix products, segment_terms_of(): jnp.einsum('fhrk,rkc->fhrc', picked_rows.astype(jnp.float32), trig_values...  23.8 us
    another operation x1, local copies, waits for them, and re-layouts, cycle_table(): jnp.stack([jnp.cos(angles) * factor, -jnp.sin(angles) * factor], -1)  20.1 us
    another operation x1, other arithmetic, cycle_table(): jnp.stack([jnp.cos(angles) * factor, -jnp.sin(angles) * factor], -1)  12.5 us
    gather x1, local copies, waits for them, and re-layouts, shards(): jnp.take(grid, packer_order, axis=0)  7.74 us
    pmax x1, blocking collectives, shards(): highest = lax.pmax(local_high, 'ns')  6.78 us
    pmin x1, blocking collectives, shards(): lowest = lax.pmin(local_low, 'ns')  6.26 us
  transfers between devices with their start and end apart: 2, of which 2 were waited for; matrix products, arithmetic and copies ran while one was open for 1% of the time, Pallas kernels for 0%

commit v1 on v0

v1 whole, which is shorter than its diff:
```python
import functools
import jax
import jax.numpy as jnp
from jax import lax
from jax.experimental import pallas as pl
from jax.experimental.pallas import tpu as pltpu
from jax.sharding import PartitionSpec as P

ROWS = 16
LANES = 128


def sincos_of(product, length):
    quarter = length * 0.25
    turns = jnp.round(product * (1.0 / quarter))
    rest = product - turns * quarter
    y = rest * (6.283185307179586 / length)
    y2 = y * y
    sine = y * (1.0 + y2 * (-0.16666654611 + y2 * (0.0083321608736 + y2 * -0.00019515295891)))
    cosine = 1.0 + y2 * (-0.5 + y2 * (0.041666645683 + y2 * (-0.0013887316255 + y2 * 2.4433157118e-05)))
    quadrant = turns.astype(jnp.int32)
    odd = (quadrant & 1) == 1
    upper = (quadrant & 2) == 2
    c = jnp.where(odd, sine, cosine)
    s = jnp.where(odd, cosine, sine)
    minus_c = odd != upper
    return jnp.where(minus_c, -c, c), jnp.where(upper, s, -s)


def fourier_kernel(sizes, order_ref, band_ref, wave_ref, grid_ref, out_ref, hi_ref, lo_ref, acc_ref):
    slots, pairs, rows, segment, truncation, row_axis, point_axis = sizes
    width = 4 * pairs
    blocks = pl.cdiv(segment, LANES)
    step = pl.program_id(0)
    first_row = lax.axis_index(row_axis) * rows + step * ROWS
    first = lax.axis_index(point_axis) * segment

    sub = lax.broadcasted_iota(jnp.int32, (ROWS, LANES), 0)
    lane = lax.broadcasted_iota(jnp.int32, (ROWS, LANES), 1)
    cycle = jnp.zeros((ROWS, LANES), jnp.int32)
    for r in range(ROWS):
        cycle = jnp.where(sub == r, band_ref[first_row + r], cycle)
    length_i = 20 + 4 * cycle
    length = length_i.astype(jnp.float32)
    points = (first + lane).astype(jnp.float32)

    numbers = []
    for p in range(pairs):
        numbers += [wave_ref[p], truncation - wave_ref[p]]
    number_lane = jnp.zeros((ROWS, LANES), jnp.int32)
    for j, number in enumerate(numbers):
        number_lane = jnp.where(lane == j, number, number_lane)
    hop_c, hop_s = sincos_of((number_lane * LANES).astype(jnp.float32), length)

    for j, number in enumerate(numbers):
        c0, s0 = sincos_of(points * number.astype(jnp.float32), length)
        hc = hop_c[:, j : j + 1]
        hs = hop_s[:, j : j + 1]
        twice = jnp.broadcast_to(hc + hc, (ROWS, LANES))
        for a in range(blocks):
            if a == 0:
                c, s = c0, s0
            elif a == 1:
                c, s = c0 * hc - s0 * hs, c0 * hs + s0 * hc
                cp, sp = c0, s0
            else:
                c, s, cp, sp = twice * c - cp, twice * s - sp, c, s
            for e, v in ((0, c), (1, s)):
                hi = v.astype(jnp.bfloat16)
                lo = (v - hi.astype(jnp.float32)).astype(jnp.bfloat16)
                at = (2 * j + e) * ROWS
                hi_ref[at : at + ROWS, a * LANES : (a + 1) * LANES] = hi
                lo_ref[at : at + ROWS, a * LANES : (a + 1) * LANES] = lo

    inside = []
    for a in range(blocks):
        m = (first + a * LANES + lane) < length_i
        if (a + 1) * LANES > segment:
            m = m & (lane < segment - a * LANES)
        inside.append(m)
    pieces = []
    for s in range(slots):
        which = order_ref[s]
        for h in range(2):
            row = grid_ref[which, h]
            cols = []
            for a in range(blocks):
                n = min(LANES, segment - a * LANES)
                cols.append(row[:, a * LANES : a * LANES + n])
            if segment % LANES:
                cols[-1] = jnp.concatenate([cols[-1], jnp.zeros((ROWS, LANES - segment % LANES), row.dtype)], 1)
            pieces.append(jnp.concatenate([jnp.where(m, v, jnp.zeros_like(v)) for m, v in zip(inside, cols)], 1))
    values = jnp.concatenate(pieces, 0)
    dims = (((1,), (1,)), ((), ()))
    product = lax.dot_general(values, hi_ref[...], dims, preferred_element_type=jnp.float32)
    product += lax.dot_general(values, lo_ref[...], dims, preferred_element_type=jnp.float32)

    inverse = 1.0 / length
    inverse = jnp.concatenate([inverse] * (width * ROWS // LANES), 1)
    wide = (ROWS, width * ROWS)
    own = lax.broadcasted_iota(jnp.int32, wide, 0) == lax.broadcasted_iota(jnp.int32, wide, 1) % ROWS
    pick = jnp.where(own, inverse, 0.0)
    picked = jnp.sum(product.reshape(slots * 2, ROWS, width * ROWS) * pick[None], axis=1)
    acc_ref[step] = picked

    @pl.when(step == pl.num_programs(0) - 1)
    def _():
        steps = rows // ROWS
        for p in range(pairs):
            parts = []
            for q in range(4):
                at = (4 * p + q) * ROWS
                parts += [acc_ref[g, :, at : at + ROWS] for g in range(steps)]
            whole = jnp.concatenate(parts, 1)
            for s in range(slots):
                out_ref[s, p] = whole[2 * s : 2 * s + 2]


def fourier(grid, band_rows, wave_pairs, packer_order, truncation, row_axis, point_axis):
    slots, hemispheres, rows, segment = grid.shape
    pairs = wave_pairs.shape[0]
    sizes = (slots, pairs, rows, segment, truncation, row_axis, point_axis)
    padded = pl.cdiv(segment, LANES) * LANES
    width = 4 * pairs
    return pl.pallas_call(
        functools.partial(fourier_kernel, sizes),
        grid_spec=pltpu.PrefetchScalarGridSpec(
            num_scalar_prefetch=3,
            grid=(rows // ROWS,),
            in_specs=[pl.BlockSpec((slots, hemispheres, ROWS, segment), lambda i, *_: (0, 0, i, 0))],
            out_specs=pl.BlockSpec((slots, pairs, 2, 4 * rows), lambda i, *_: (0, 0, 0, 0)),
            scratch_shapes=[
                pltpu.VMEM((width * ROWS, padded), jnp.bfloat16),
                pltpu.VMEM((width * ROWS, padded), jnp.bfloat16),
                pltpu.VMEM((rows // ROWS, slots * 2, width * ROWS), jnp.float32),
            ],
        ),
        out_shape=jax.ShapeDtypeStruct((slots, pairs, 2, 4 * rows), jnp.float32),
        name="fourier_segment",
    )(packer_order, band_rows, wave_pairs, grid)


def legendre_kernel(sizes, order_ref, bits_ref, power_ref, wave_ref, *refs):
    parts, rows, truncation, levels, slot, row_axis, point_axis, slots_here, pair, pairs_here = sizes
    piece_refs, (upper_ref, lower_ref, scaled_ref, stats_ref, band_ref, values_ref) = refs[:parts], refs[parts:]
    me = lax.axis_index(row_axis)
    for d in range(parts):
        band_ref[lax.rem(me + parts - d, parts)] = piece_refs[d][...]
    for b in range(parts):
        north, south = band_ref[b, 0:1, :], band_ref[b, 1:2, :]
        even, odd = north + south, north - south
        for q in range(4):
            values_ref[q : q + 1, b * rows : (b + 1) * rows] = even[:, q * rows : (q + 1) * rows]
            values_ref[4 + q : 5 + q, b * rows : (b + 1) * rows] = odd[:, q * rows : (q + 1) * rows]
    values = values_ref[...]
    high = values.astype(jnp.bfloat16)
    low = (values - high.astype(jnp.float32)).astype(jnp.bfloat16)
    dims = (((1,), (1,)), ((), ()))
    first = lax.dot_general(
        jnp.concatenate([high, low], 0), upper_ref[...], dims, preferred_element_type=jnp.float32
    )
    second = lax.dot_general(high, lower_ref[...], dims, preferred_element_type=jnp.float32)
    result = first[0:8] + first[8:16] + second

    wave = wave_ref[me * pairs_here + pair]
    columns = lax.broadcasted_iota(jnp.int32, (1, result.shape[1]), 1)
    first_part = columns <= truncation - wave
    shifted = columns - (truncation - wave + 1)
    parity = jnp.where(first_part, columns, shifted) & 1
    even_parity = parity == 0
    chosen = jnp.where(
        first_part,
        jnp.where(even_parity, result[0:2], result[4:6]),
        jnp.where(even_parity, result[2:4], result[6:8]),
    )
    degree = jnp.where(first_part, wave + columns, columns - 1).astype(jnp.float32)
    kind = order_ref[lax.axis_index(point_axis) * slots_here + slot] // levels
    weight = jnp.exp(power_ref[kind] * jnp.log(degree * (degree + 1.0) + 2.0))
    scaled = chosen * weight
    scaled_ref[...] = scaled
    lane = lax.broadcasted_iota(jnp.int32, (1, LANES), 1)
    bits = jnp.full((1, LANES), bits_ref[kind], jnp.int32)
    spread = ((1 << bits).astype(jnp.float32) - 1.0) / 4096.0
    stats_ref[...] = jnp.where(lane == 0, jnp.max(scaled), jnp.where(lane == 1, -jnp.min(scaled), spread))


def legendre_part(pieces, upper, lower, order, bits, power, waves, levels, truncation, slot, pair, counts, axes):
    parts = len(pieces)
    rows = pieces[0].shape[1] // 4
    columns = upper.shape[0]
    sizes = (parts, rows, truncation, levels, slot, *axes, counts[0], pair, counts[1])
    scalar = pl.BlockSpec(memory_space=pltpu.SMEM)
    vector = pl.BlockSpec(memory_space=pltpu.VMEM)
    return pl.pallas_call(
        functools.partial(legendre_kernel, sizes),
        in_specs=[scalar] * 4 + [vector] * (parts + 2),
        out_specs=[vector] * 2,
        scratch_shapes=[
            pltpu.VMEM((parts, 2, 4 * rows), jnp.float32),
            pltpu.VMEM((8, parts * rows), jnp.float32),
        ],
        out_shape=[jax.ShapeDtypeStruct((2, columns), jnp.float32), jax.ShapeDtypeStruct((1, LANES), jnp.float32)],
        name="legendre_pair",
    )(order, bits, power, waves, *pieces, upper, lower)


def rounds(value_of, axis):
    count = lax.axis_size(axis)
    me = lax.axis_index(axis)
    moved = [value_of(me)]
    for d in range(1, count):
        to = lax.rem(me + d, count)
        moved.append(lax.ppermute(value_of(to), axis, [(i, (i + d) % count) for i in range(count)]))
    return moved


def shards(grid, band_rows, wave_pairs, packer_order, field_bits, field_power, legendre):
    total_slots = grid.shape[0]
    rows = grid.shape[2]
    sources = lax.axis_size("ew")
    bands = lax.axis_size("ns")
    fl_dev = total_slots // sources
    pair_dev = legendre.shape[0]
    pairs = wave_pairs.shape[0]
    truncation = legendre.shape[2] - 2
    levels = total_slots // field_bits.shape[0]

    terms = fourier(grid, band_rows, wave_pairs, packer_order, truncation, "ns", "ew")
    arrived = lax.all_to_all(terms, "ew", 0, 0, tiled=True)
    summed = jnp.sum(arrived.reshape(sources, fl_dev, pairs, 2, 4 * rows), axis=0)

    turned = jnp.transpose(legendre, (0, 2, 1))
    upper = lax.reduce_precision(turned, 8, 7)
    lower = (turned - upper).astype(jnp.bfloat16)
    upper = upper.astype(jnp.bfloat16)

    outs = []
    for slot in range(fl_dev):
        for pair in range(pair_dev):
            pieces = rounds(
                lambda to: lax.dynamic_index_in_dim(summed[slot], to * pair_dev + pair, 0, keepdims=False), "ns"
            )
            outs.append(
                legendre_part(
                    pieces, upper[pair], lower[pair], packer_order, field_bits, field_power, wave_pairs,
                    levels, truncation, slot, pair, (fl_dev, pair_dev), ("ns", "ew"),
                )
            )
    packed = []
    for slot in range(fl_dev):
        mine = outs[slot * pair_dev : (slot + 1) * pair_dev]
        stats = mine[0][1]
        for _, other in mine[1:]:
            stats = jnp.maximum(stats, other)
        everyone = rounds(lambda to: stats, "ns")
        for other in everyone[1:]:
            stats = jnp.maximum(stats, other)
        highest, lowest, spread = stats[0, 0], -stats[0, 1], stats[0, 2]
        span = highest - lowest + 1e-06
        packed.append(jnp.stack([(scaled - lowest) / span * spread for scaled, _ in mine]))
    return jnp.stack(packed)


def solution(mesh):
    return jax.shard_map(
        shards,
        mesh=mesh,
        in_specs=(P(None, None, "ns", "ew"), P(), P(), P(), P(), P(), P("ns", None, None)),
        out_specs=P("ew", "ns", None, None),
        check_vma=False,
    )
```

time: 292 us -> 57.6 us (0.20)
  other arithmetic: 132 us -> 5.8 us
  waiting for transfers between devices: 60.4 us -> 14.3 us
  local copies, waits for them, and re-layouts: 34.3 us -> 1.86 us
  matrix products: 28.6 us -> 0 us
  Pallas kernels: 0 us -> 23.4 us
  between operations: 19.4 us -> 1.22 us
  blocking collectives: 13 us -> 0 us
  starting transfers between devices: 3.27 us -> 10.4 us
    mul x3 -> x0, other arithmetic: 108 us -> none  [the longest x1 107 us: cycle_table(): jnp.cos(angles) * factor]
    reduce_scatter x1 -> x0, waiting for transfers between devices: 59.2 us -> none  [shards(): lax.psum_scatter(segment_terms_of(jnp.take(grid, packer_order, axis=0), t...]
    dot_general x2 -> x0, matrix products: 28.6 us -> none  [the longest x1 23.8 us: segment_terms_of(): jnp.einsum('fhrk,rkc->fhrc', picked_rows.astype(jnp.float32), trig_values...]
    pallas_call x0 -> x2, Pallas kernels: none -> 23.4 us  [the longest x1 19.7 us: fourier(): pl.pallas_call(functools.partial(fourier_kernel, sizes), grid_spec=pltpu....]
    another operation x2 -> x0, local copies, waits for them, and re-layouts: 20.2 us -> none  [the longest x1 20.1 us: cycle_table(): jnp.stack([jnp.cos(angles) * factor, -jnp.sin(angles) * factor], -1)]
    another operation x3 -> x1, other arithmetic: 13.8 us -> 1.92 us  [shards(): return jnp.stack(packed)]
    all_to_all x1, waiting for transfers between devices: 1.27 us -> 10.4 us  [shards(): arrived = lax.all_to_all(terms, 'ew', 0, 0, tiled=True)]
    gather x1 -> x0, local copies, waits for them, and re-layouts: 7.74 us -> none  [shards(): jnp.take(grid, packer_order, axis=0)]
  transfers between devices with their start and end apart: 2 -> 7, of which waited for: 2 -> 4; matrix products, arithmetic and copies ran while one was open for 1% -> 4% of each run, Pallas kernels for 0% -> 0%
where the time goes in v1:
time: 57.6 us; the launch traced here: 57 us
  Pallas kernels  23.4 us (41%)
  waiting for transfers between devices  14.3 us (25%)
  starting transfers between devices  10.4 us (18%)
  other arithmetic  5.8 us (10%)
  local copies, waits for them, and re-layouts  1.86 us (3%)
  between operations  1.22 us (2%)
    pallas_call x1, Pallas kernels, fourier(): pl.pallas_call(functools.partial(fourier_kernel, sizes), grid_spec=pltpu....  19.7 us
    all_to_all x1, waiting for transfers between devices, shards(): arrived = lax.all_to_all(terms, 'ew', 0, 0, tiled=True)  10.4 us
    all_to_all x1, starting transfers between devices, shards(): arrived = lax.all_to_all(terms, 'ew', 0, 0, tiled=True)  7.28 us
    ppermute x6, waiting for transfers between devices, rounds(): lax.ppermute(value_of(to), axis, [(i, (i + d) % count) for i in range(cou...  3.94 us
    pallas_call x1, Pallas kernels, legendre_part(): pl.pallas_call(functools.partial(legendre_kernel, sizes), in_specs=[scala...  3.7 us
    ppermute x6, starting transfers between devices, rounds(): lax.ppermute(value_of(to), axis, [(i, (i + d) % count) for i in range(cou...  3.12 us
    squeeze x1, other arithmetic, shards(): lower[pair]  2.18 us
    another operation x1, other arithmetic, shards(): return jnp.stack(packed)  1.92 us
  transfers between devices with their start and end apart: 7, of which 4 were waited for; matrix products, arithmetic and copies ran while one was open for 4% of the time, Pallas kernels for 0%

profile of v1, /device:TPU:0, one launch (start us, length us, event | category | flops | bytes accessed | tf_op | source)
XLA Modules:
  0.0 57.0 jit_solution(4776224557142334856)
XLA Ops:
  0.0 0.0 copy-start
  0.0 19.7 %fourier_segment.1 = f32[8,4,2,1280]{3,2,1,0:T(2,128)} custom-call(s32[8]{0:T(128)} %order_ref.3, s32[1280]{0:T(1024)} %band_ref.1, s32[4]{0:T(128)} %wave_ref.3, bf16[8,2,320,642]{3,2,1,0:T(8,128)(2,1)} %grid_ref.1), custom_call_target="tpu_custom_call" | custom-call | tf_op jit(solution)/shard_map/fourier_segment/pallas_call | solution.py:125
  19.7 7.3 %all-to-all-start = ((f32[8,4,2,1280]{3,2,1,0:T(2,128)}), f32[8,4,2,1280]{3,2,1,0:T(2,128)}, u32[]{:S(2)}, u32[]{:S(2)}) async-start(f32[8,4,2,1280]{3,2,1,0:T(2,128)} %fourier_segment.1), calls=%async_computation | async-start | bytes 655360 | tf_op jit(solution)/shard_map/all_to_all | solution.py:229
  27.0 10.4 %all-to-all-done = f32[8,4,2,1280]{3,2,1,0:T(2,128)} async-done(((f32[8,4,2,1280]{3,2,1,0:T(2,128)}), f32[8,4,2,1280]{3,2,1,0:T(2,128)}, u32[]{:S(2)}, u32[]{:S(2)}) %all-to-all-start) | async-done | bytes 327712 | tf_op jit(solution)/shard_map/all_to_all | solution.py:229
  37.4 1.1 %reduce_sum.9 = f32[4,2,1280]{2,1,0:T(2,128)S(1)} reduce(f32[8,4,2,1280]{3,2,1,0:T(2,128)} %all-to-all-done, f32[]{:T(128)} %constant.29.clone.1), dimensions={0}, to_apply=%region_0.0 | reduce | flops 71680 | bytes 368644 | tf_op jit(solution)/shard_map/reduce_sum | solution.py:230
  38.5 0.6 %dynamic-slice_bitcast_fusion = (f32[2,1280]{1,0:T(2,128)S(1)}, f32[2,1280]{1,0:T(2,128)S(1)}, f32[2,1280]{1,0:T(2,128)S(1)}, f32[2,1280]{1,0:T(2,128)}) fusion(f32[4,2,1280]{2,1,0:T(2,128)S(1)} %reduce_sum.9, s32[]{:T(128)S(6)} %select_n.16, s32[]{:T(128)S(6)} %select_n.15, s32[]{:T(128)S(6)} %select_n.14, s32[]{:T(128)S(6)} %select_n.13), kind=kLoop, calls=%fused_computation.5 | loop fusion | bytes 81936 | tf_op jit(solution)/shard_map/jit(dynamic_index_in_dim)/squeeze | solution.py:241
  39.1 0.0 collective-permute-start.2
  39.1 1.5 %collective-permute-start.1 = (f32[2,1280]{1,0:T(2,128)S(1)}, f32[2,1280]{1,0:T(2,128)S(1)}, u32[]{:S(2)}, u32[]{:S(2)}) collective-permute-start(f32[2,1280]{1,0:T(2,128)S(1)} %get-tuple-element.12), channel_id=1, source_target_pairs={{0,2},{1,3},{2,0},{3,1},{4,6},{5,7},{6,4},{7,5},{8,10},{9,11},{10,... | collective-permute-start | bytes 30728 | tf_op jit(solution)/shard_map/ppermute | solution.py:213
  40.6 0.2 collective-permute-start
  40.8 0.0 copy-done
  40.8 2.2 %fusion.1 = (bf16[649,1280]{1,0:T(8,128)(2,1)}, bf16[649,1280]{1,0:T(8,128)(2,1)}) fusion(f32[1,1280,649]{1,0,2:T(1,128)S(1)} %copy-done), kind=kLoop, calls=%fused_computation.3 | loop fusion | flops 3322880 | bytes 6645760 | tf_op jit(solution)/shard_map/squeeze | solution.py:245
  43.0 0.0 collective-permute-done.2.refs_3_
  43.0 0.0 copy-start.1
  43.0 0.0 collective-permute-done.1.refs_2_
  43.0 0.0 copy-start.2
  43.0 0.7 %collective-permute-done.refs_1_ = f32[2,1280]{1,0:T(2,128)S(1)} collective-permute-done((f32[2,1280]{1,0:T(2,128)S(1)}, f32[2,1280]{1,0:T(2,128)S(1)}, u32[]{:S(2)}, u32[]{:S(2)}) %collective-permute-start) | collective-permute-done | bytes 10272 | tf_op jit(solution)/shard_map/ppermute | solution.py:213
  43.7 0.0 copy-start.3
  43.7 0.0 copy-done.1
  43.7 0.0 copy-done.2
  43.7 0.6 %copy-done.3 = f32[2,1280]{1,0:T(2,128)} copy-done((f32[2,1280]{1,0:T(2,128)}, f32[2,1280]{1,0:T(2,128)S(1)}, u32[]{:S(2)}) %copy-start.3) | copy-done | bytes 10264
  44.3 3.7 %legendre_pair.1 = (f32[2,649]{1,0:T(2,128)}, f32[1,128]{1,0:T(1,128)}) custom-call(s32[8]{0:T(128)} %order_ref.3, s32[4]{0:T(128)} %bits_ref.1, f32[4]{0:T(128)} %power_ref.1, s32[4]{0:T(128)} %wave_ref.3, f32[2,1280]{1,0:T(2,128)} %get-tuple-element.14.refs_0_, f32[2,1280]{1,0:T(2,128)} %copy-done.3, f32[2,1280]{1,0:T(2,128)} %copy-done.2, ...), custom_call_target="tpu_custom_call" | custom-call | tf_op jit(solution)/shard_map/legendre_pair/pallas_call | solution.py:194
  48.0 0.9 %collective-permute-start.5 = (f32[1,128]{1,0:T(1,128)}, f32[1,128]{1,0:T(1,128)S(1)}, u32[]{:S(2)}, u32[]{:S(2)}) collective-permute-start(f32[1,128]{1,0:T(1,128)} %get-tuple-element.8), channel_id=1, source_target_pairs={{0,3},{1,0},{2,1},{3,2},{4,7},{5,4},{6,5},{7,6},{8,11},{9,8},{10,9... | collective-permute-start | bytes 1544 | tf_op jit(solution)/shard_map/ppermute | solution.py:213
  48.8 0.5 collective-permute-start.4
  49.3 0.0 collective-permute-start.3
  49.4 1.0 %collective-permute-done.5 = f32[1,128]{1,0:T(1,128)S(1)} collective-permute-done((f32[1,128]{1,0:T(1,128)}, f32[1,128]{1,0:T(1,128)S(1)}, u32[]{:S(2)}, u32[]{:S(2)}) %collective-permute-start.5) | collective-permute-done | bytes 544 | tf_op jit(solution)/shard_map/ppermute | solution.py:213
  50.3 2.3 %collective-permute-done.4 = f32[1,128]{1,0:T(1,128)S(1)} collective-permute-done((f32[1,128]{1,0:T(1,128)}, f32[1,128]{1,0:T(1,128)S(1)}, u32[]{:S(2)}, u32[]{:S(2)}) %collective-permute-start.4) | collective-permute-done | bytes 544 | tf_op jit(solution)/shard_map/ppermute | solution.py:213
  52.6 0.0 collective-permute-done.3
  52.6 0.6 %maximum_maximum_fusion = f32[1,128]{1,0:T(1,128)S(1)} fusion(f32[1,128]{1,0:T(1,128)S(1)} %collective-permute-done.5, f32[1,128]{1,0:T(1,128)S(1)} %collective-permute-done.4, f32[1,128]{1,0:T(1,128)} %get-tuple-element.8, f32[1,128]{1,0:T(1,128)S(1)} %collective-permute-done.3), kind=kLoop, calls=%fused_computation.10 | loop fusion | flops 384 | bytes 2560 | tf_op jit(solution)/shard_map/max | solution.py:257
  53.2 0.6 %fusion.3 = (f32[1,1]{1,0:T(1,128)}, f32[1,1]{1,0:T(1,128)}, f32[1,1]{1,0:T(1,128)}) fusion(f32[1,128]{1,0:T(1,128)S(1)} %maximum_maximum_fusion), kind=kLoop, calls=%fused_computation.11 | loop fusion | bytes 24 | tf_op jit(solution)/shard_map/slice | solution.py:258
  55.1 1.9 %multiply_bitcast_fusion = f32[1,1,2,649]{3,2,1,0:T(2,128)} fusion(f32[2,649]{1,0:T(2,128)} %get-tuple-element.7, f32[]{:T(128)} %bitcast.9, f32[]{:T(128)S(6)} %add.32, f32[]{:T(128)} %bitcast.7), kind=kLoop, calls=%fused_computation.9 | loop fusion | flops 3894 | bytes 10396 | tf_op jit(solution)/shard_map/stack;stack | solution.py:261
Async XLA Ops:
  0.0 40.8 %copy-start = (f32[1,1280,649]{1,0,2:T(1,128)S(1)}, f32[1,1280,649]{1,0,2:T(1,128)}, u32[]{:S(2)}) copy-start(f32[1,1280,649]{1,0,2:T(1,128)} %param.13) | copy-start | bytes 9968644
  19.7 17.7 %all-to-all-start = ((f32[8,4,2,1280]{3,2,1,0:T(2,128)}), f32[8,4,2,1280]{3,2,1,0:T(2,128)}, u32[]{:S(2)}, u32[]{:S(2)}) async-start(f32[8,4,2,1280]{3,2,1,0:T(2,128)} %fourier_segment.1), calls=%async_computation | async-start | bytes 655360 | tf_op jit(solution)/shard_map/all_to_all | solution.py:229
  39.1 3.9 %collective-permute-start.2 = (f32[2,1280]{1,0:T(2,128)S(1)}, f32[2,1280]{1,0:T(2,128)S(1)}, u32[]{:S(2)}, u32[]{:S(2)}) collective-permute-start(f32[2,1280]{1,0:T(2,128)S(1)} %get-tuple-element.11), channel_id=1, source_target_pairs={{0,3},{1,0},{2,1},{3,2},{4,7},{5,4},{6,5},{7,6},{8,11},{9,8},{10,9... | collective-permute-start | bytes 30728 | tf_op jit(solution)/shard_map/ppermute | solution.py:213
  39.1 3.9 %collective-permute-start.1 = (f32[2,1280]{1,0:T(2,128)S(1)}, f32[2,1280]{1,0:T(2,128)S(1)}, u32[]{:S(2)}, u32[]{:S(2)}) collective-permute-start(f32[2,1280]{1,0:T(2,128)S(1)} %get-tuple-element.12), channel_id=1, source_target_pairs={{0,2},{1,3},{2,0},{3,1},{4,6},{5,7},{6,4},{7,5},{8,10},{9,11},{10,... | collective-permute-start | bytes 30728 | tf_op jit(solution)/shard_map/ppermute | solution.py:213
  40.6 3.1 %collective-permute-start = (f32[2,1280]{1,0:T(2,128)S(1)}, f32[2,1280]{1,0:T(2,128)S(1)}, u32[]{:S(2)}, u32[]{:S(2)}) collective-permute-start(f32[2,1280]{1,0:T(2,128)S(1)} %get-tuple-element.13), channel_id=1, source_target_pairs={{0,1},{1,2},{2,3},{3,0},{4,5},{5,6},{6,7},{7,4},{8,9},{9,10},{10,1... | collective-permute-start | bytes 30728 | tf_op jit(solution)/shard_map/ppermute | solution.py:213
  43.0 0.7 %copy-start.1 = (f32[2,1280]{1,0:T(2,128)}, f32[2,1280]{1,0:T(2,128)S(1)}, u32[]{:S(2)}) copy-start(f32[2,1280]{1,0:T(2,128)S(1)} %collective-permute-done.2.refs_3_) | copy-start | bytes 30724
  43.0 0.7 %copy-start.2 = (f32[2,1280]{1,0:T(2,128)}, f32[2,1280]{1,0:T(2,128)S(1)}, u32[]{:S(2)}) copy-start(f32[2,1280]{1,0:T(2,128)S(1)} %collective-permute-done.1.refs_2_) | copy-start | bytes 30724
  43.7 0.6 %copy-start.3 = (f32[2,1280]{1,0:T(2,128)}, f32[2,1280]{1,0:T(2,128)S(1)}, u32[]{:S(2)}) copy-start(f32[2,1280]{1,0:T(2,128)S(1)} %collective-permute-done.refs_1_) | copy-start | bytes 30724
  48.0 2.4 %collective-permute-start.5 = (f32[1,128]{1,0:T(1,128)}, f32[1,128]{1,0:T(1,128)S(1)}, u32[]{:S(2)}, u32[]{:S(2)}) collective-permute-start(f32[1,128]{1,0:T(1,128)} %get-tuple-element.8), channel_id=1, source_target_pairs={{0,3},{1,0},{2,1},{3,2},{4,7},{5,4},{6,5},{7,6},{8,11},{9,8},{10,9... | collective-permute-start | bytes 1544 | tf_op jit(solution)/shard_map/ppermute | solution.py:213
  48.8 3.8 %collective-permute-start.4 = (f32[1,128]{1,0:T(1,128)}, f32[1,128]{1,0:T(1,128)S(1)}, u32[]{:S(2)}, u32[]{:S(2)}) collective-permute-start(f32[1,128]{1,0:T(1,128)} %get-tuple-element.8), channel_id=1, source_target_pairs={{0,2},{1,3},{2,0},{3,1},{4,6},{5,7},{6,4},{7,5},{8,10},{9,11},{10,... | collective-permute-start | bytes 1544 | tf_op jit(solution)/shard_map/ppermute | solution.py:213
  49.3 3.3 %collective-permute-start.3 = (f32[1,128]{1,0:T(1,128)}, f32[1,128]{1,0:T(1,128)S(1)}, u32[]{:S(2)}, u32[]{:S(2)}) collective-permute-start(f32[1,128]{1,0:T(1,128)} %get-tuple-element.8), channel_id=1, source_target_pairs={{0,1},{1,2},{2,3},{3,0},{4,5},{5,6},{6,7},{7,4},{8,9},{9,10},{10,1... | collective-permute-start | bytes 1544 | tf_op jit(solution)/shard_map/ppermute | solution.py:213
